TPU v7x, 32 devices: a whole 2x2x4 slice. The times are simulated.
32 devices in a mesh: rows: 4 (over y, x), ffn: 8 (over z, core).
Axes of the slice: x: 2, y: 2, z: 4, core: 2. Of those that a mesh axis runs over, the one named last changes fastest.
Arguments:
- tokens: bfloat16 [32768, 1024], P(('rows', 'ffn')), may hold values from -6 to 6
- lengths: int32 [32], P(('rows', 'ffn')), may hold values from 128 to 1024, as said below
- cotangent: bfloat16 [32768, 1024], P(('rows', 'ffn')), may hold values from -6 to 6
- ln_attn_gain: float32 [1024], replicated, may hold values from 0.1 to 1.9
- ln_attn_bias: float32 [1024], replicated, may hold values from -1.75 to 1.75
- w_query: bfloat16 [1024, 1024], P(('rows', 'ffn')), may hold values from -0.1875 to 0.1875
- query_bias: float32 [1024], replicated, may hold values from -3 to 3
- w_key: bfloat16 [1024, 1024], P(('rows', 'ffn')), may hold values from -0.1875 to 0.1875
- w_value: bfloat16 [1024, 1024], P(('rows', 'ffn')), may hold values from -0.1875 to 0.1875
- value_bias: float32 [1024], replicated, may hold values from -3 to 3
- head_scale: float32 [16], replicated, may hold values from 0.3 to 3
- w_out: bfloat16 [1024, 1024], P(('rows', 'ffn')), may hold values from -0.1875 to 0.1875
- out_bias: float32 [1024], replicated, may hold values from -3 to 3
- post_gain: float32 [1024], replicated, may hold values from 0.1 to 1.9
- post_bias: float32 [1024], replicated, may hold values from -1.75 to 1.75
- ffn_gain: float32 [1024], replicated, may hold values from 0.1 to 1.9
- ffn_bias: float32 [1024], replicated, may hold values from -1.75 to 1.75
- w_up: bfloat16 [1024, 4096], P('rows', 'ffn'), may hold values from -1 to 1
- up_bias: float32 [4096], replicated, may hold values from -3 to 3
- mid_gain: float32 [4096], replicated, may hold values from 0.1 to 1.9
- mid_bias: float32 [4096], replicated, may hold values from -1.75 to 1.75
- w_down: bfloat16 [1024, 4096], P('rows', 'ffn'), may hold values from -0.09375 to 0.09375
- down_bias: float32 [1024], replicated, may hold values from -3 to 3
Outputs:
- result: float32 [32768, 1024], P(('rows', 'ffn'))
- grad_tokens: float32 [32768, 1024], P(('rows', 'ffn'))
- grad_ln_attn_gain: float32 [1024], replicated
- grad_ln_attn_bias: float32 [1024], replicated
- grad_w_query: float32 [1024, 1024], P(('rows', 'ffn'))
- grad_query_bias: float32 [1024], replicated
- grad_w_key: float32 [1024, 1024], P(('rows', 'ffn'))
- grad_w_value: float32 [1024, 1024], P(('rows', 'ffn'))
- grad_value_bias: float32 [1024], replicated
- grad_head_scale: float32 [16], replicated
- grad_w_out: float32 [1024, 1024], P(('rows', 'ffn'))
- grad_out_bias: float32 [1024], replicated
- grad_post_gain: float32 [1024], replicated
- grad_post_bias: float32 [1024], replicated
- grad_ffn_gain: float32 [1024], replicated
- grad_ffn_bias: float32 [1024], replicated
- grad_w_up: float32 [1024, 4096], P('rows', 'ffn')
- grad_up_bias: float32 [4096], P('ffn')
- grad_mid_gain: float32 [4096], P('ffn')
- grad_mid_bias: float32 [4096], P('ffn')
- grad_w_down: float32 [1024, 4096], P('rows', 'ffn')
- grad_down_bias: float32 [1024], replicated
Inputs may be any that keep to these rules, and one draw needn't show every extreme that they name: `lengths`: each sequence has between 128 and 1024 valid tokens, at the start of its slots; some sequence has exactly 1024.
All inputs are finite; a program needn't handle non-finite values.
Results may differ from a plain program's by a relative error of at most 0.013.
Values may be sent and summed in bfloat16 or wider, within the bound.
A program may use at most 320 MiB of HBM per device.

v0:
```python
import jax
import jax.numpy as jnp
from jax import lax
from jax.sharding import PartitionSpec as P

epsilon = 1e-05
masked_score = -1e30


def layer_norm(values, gain, shift):
    center = jnp.mean(values, axis=-1, keepdims=True)
    centered = values - center
    spread = jnp.mean(centered * centered, axis=-1, keepdims=True)
    return centered * lax.rsqrt(spread + epsilon) * gain + shift


def exact_gelu(values):
    return jax.nn.gelu(values, approximate=False)


def plain_dot(left, right):
    return jnp.dot(left, right, preferred_element_type=jnp.float32)


def contract_rows(left, right):
    return lax.dot_general(
        left, right, (((0,), (0,)), ((), ())), preferred_element_type=jnp.float32
    )


def contract_cols(left, right):
    return lax.dot_general(
        left, right, (((1,), (1,)), ((), ())), preferred_element_type=jnp.float32
    )


def block_scores(queries, key_rows, first, block_rows, length):
    rows_here = lax.dynamic_slice_in_dim(queries, first, block_rows, 0)
    factor = queries.shape[-1] ** (-0.5)
    scores = (
        jnp.einsum("qhd,khd->hqk", rows_here, key_rows, preferred_element_type=jnp.float32) * factor
    )
    key_pos = jnp.arange(key_rows.shape[0])
    query_pos = first + jnp.arange(block_rows)
    allowed = (key_pos[None, :] <= query_pos[:, None]) & (key_pos[None, :] < length)
    return (rows_here, jnp.where(allowed[None], scores, masked_score))


def attend_forward(queries, key_rows, value_rows, length, block_rows):

    def one_block(first):
        rows_here, scores = block_scores(queries, key_rows, first, block_rows, length)
        peak = jnp.max(scores, axis=-1, keepdims=True)
        weights = jnp.exp(scores - peak)
        totals = jnp.sum(weights, axis=-1, keepdims=True)
        probs = (weights / totals).astype(jnp.bfloat16)
        context = jnp.einsum("hqk,khd->qhd", probs, value_rows, preferred_element_type=jnp.float32)
        return (context, peak[..., 0] + jnp.log(totals[..., 0]))

    firsts = jnp.arange(queries.shape[0] // block_rows) * block_rows
    context, log_totals = lax.map(one_block, firsts)
    return (context.reshape(queries.shape), log_totals)


def attend_backward(queries, key_rows, value_rows, grad_context, log_totals, length, block_rows):
    factor = queries.shape[-1] ** (-0.5)

    def one_block(carry, inputs_here):
        grad_keys, grad_values = carry
        first, block_log = inputs_here
        rows_here, scores = block_scores(queries, key_rows, first, block_rows, length)
        grad_rows = lax.dynamic_slice_in_dim(grad_context, first, block_rows, 0)
        probs = jnp.exp(scores - block_log[..., None])
        grad_probs = jnp.einsum(
            "qhd,khd->hqk", grad_rows, value_rows, preferred_element_type=jnp.float32
        )
        grad_values = grad_values + jnp.einsum(
            "hqk,qhd->khd",
            probs.astype(jnp.bfloat16),
            grad_rows,
            preferred_element_type=jnp.float32,
        )
        inner = jnp.sum(probs * grad_probs, axis=-1, keepdims=True)
        grad_scores = (probs * (grad_probs - inner)).astype(jnp.bfloat16)
        grad_queries = (
            jnp.einsum("hqk,khd->qhd", grad_scores, key_rows, preferred_element_type=jnp.float32)
            * factor
        )
        grad_keys = (
            grad_keys
            + jnp.einsum("hqk,qhd->khd", grad_scores, rows_here, preferred_element_type=jnp.float32)
            * factor
        )
        return ((grad_keys, grad_values), grad_queries)

    firsts = jnp.arange(queries.shape[0] // block_rows) * block_rows
    zeros_like_keys = jnp.zeros(key_rows.shape, jnp.float32)
    (grad_keys, grad_values), grad_queries = lax.scan(
        one_block, (zeros_like_keys, zeros_like_keys), (firsts, log_totals)
    )
    return (grad_queries.reshape(queries.shape), grad_keys, grad_values)


def shards(
    tokens,
    lengths,
    cotangent,
    ln_attn_gain,
    ln_attn_bias,
    w_query,
    query_bias,
    w_key,
    w_value,
    value_bias,
    head_scale,
    w_out,
    out_bias,
    post_gain,
    post_bias,
    ffn_gain,
    ffn_bias,
    w_up,
    up_bias,
    mid_gain,
    mid_bias,
    w_down,
    down_bias,
):
    seq_len, width = tokens.shape
    head_count = head_scale.shape[0]
    head_size = width // head_count
    heads_shape = (seq_len, head_count, head_size)
    block_rows = min(seq_len, 512)
    length = lengths[0]
    valid_rows = (jnp.arange(seq_len) < length)[:, None]
    inputs = tokens.astype(jnp.float32)
    full_query, full_key, full_value, full_out = (
        lax.all_gather(w_query, ("rows", "ffn"), axis=0, tiled=True),
        lax.all_gather(w_key, ("rows", "ffn"), axis=0, tiled=True),
        lax.all_gather(w_value, ("rows", "ffn"), axis=0, tiled=True),
        lax.all_gather(w_out, ("rows", "ffn"), axis=0, tiled=True),
    )
    normed, first_back = jax.vjp(layer_norm, inputs, ln_attn_gain, ln_attn_bias)
    normed_low = normed.astype(jnp.bfloat16)
    queries = (
        (plain_dot(normed_low, full_query) + query_bias).astype(jnp.bfloat16).reshape(heads_shape)
    )
    key_rows = plain_dot(normed_low, full_key).astype(jnp.bfloat16).reshape(heads_shape)
    value_rows = (
        (plain_dot(normed_low, full_value) + value_bias).astype(jnp.bfloat16).reshape(heads_shape)
    )
    context, log_totals = attend_forward(queries, key_rows, value_rows, length, block_rows)
    scaled_low = (context * head_scale[None, :, None]).reshape(seq_len, width).astype(jnp.bfloat16)
    projected = plain_dot(scaled_low, full_out) + out_bias
    branch, second_back = jax.vjp(layer_norm, projected, post_gain, post_bias)
    mixed = inputs + branch
    second, third_back = jax.vjp(layer_norm, mixed, ffn_gain, ffn_bias)
    second_low = second.astype(jnp.bfloat16)
    grad_result = jnp.where(valid_rows, cotangent.astype(jnp.float32), 0.0)
    grad_result_low = grad_result.astype(jnp.bfloat16)
    up_rows, down_rows = (
        lax.all_gather(w_up, "rows", axis=0, tiled=True),
        lax.all_gather(w_down, "rows", axis=0, tiled=True),
    )
    up_full, down_full = (
        lax.all_gather(up_rows, "ffn", axis=1, tiled=True),
        lax.all_gather(down_rows, "ffn", axis=1, tiled=True),
    )
    pre_act = plain_dot(second_low, up_full) + up_bias
    activated, gelu_back = jax.vjp(exact_gelu, pre_act)
    row_mean = jnp.mean(activated, axis=1, keepdims=True)
    inverse = lax.rsqrt(
        jnp.mean(activated * activated, axis=1, keepdims=True) - row_mean * row_mean + epsilon
    )
    unit_rows = (activated - row_mean) * inverse
    mid_low = (unit_rows * mid_gain + mid_bias).astype(jnp.bfloat16)
    ffn_part = contract_cols(mid_low, down_full)
    grad_mid = plain_dot(grad_result_low, down_full)
    grad_down_full = contract_rows(grad_result_low, mid_low)
    scaled_grad = grad_mid * mid_gain
    grad_act = (
        scaled_grad
        - jnp.mean(scaled_grad, axis=1, keepdims=True)
        - unit_rows * jnp.mean(scaled_grad * unit_rows, axis=1, keepdims=True)
    ) * inverse
    grad_pre_low = gelu_back(grad_act)[0].astype(jnp.bfloat16)
    grad_up_full = contract_rows(second_low, grad_pre_low)
    grad_second = contract_cols(grad_pre_low, up_full)
    stacked = jnp.stack(
        [
            jnp.sum(grad_pre_low.astype(jnp.float32), axis=0),
            jnp.sum(grad_mid * unit_rows, axis=0),
            jnp.sum(grad_mid, axis=0),
        ]
    )
    grad_up, grad_down, stacked_own = (
        lax.psum_scatter(grad_up_full, "ffn", scatter_dimension=1, tiled=True),
        lax.psum_scatter(grad_down_full, "ffn", scatter_dimension=1, tiled=True),
        lax.psum_scatter(stacked, "ffn", scatter_dimension=1, tiled=True),
    )
    grad_up, grad_down = (
        lax.psum_scatter(
            grad_up.astype(jnp.bfloat16), "rows", scatter_dimension=0, tiled=True
        ).astype(jnp.float32),
        lax.psum_scatter(
            grad_down.astype(jnp.bfloat16), "rows", scatter_dimension=0, tiled=True
        ).astype(jnp.float32),
    )
    grad_up_bias, grad_mid_gain, grad_mid_bias = lax.psum(
        (stacked_own[0], stacked_own[1], stacked_own[2]), "rows"
    )
    result = jnp.where(valid_rows, mixed + ffn_part + down_bias, 0.0)
    grad_mixed_in, grad_ffn_gain, grad_ffn_bias = third_back(grad_second)
    grad_mixed = grad_result + grad_mixed_in
    grad_projected, grad_post_gain, grad_post_bias = second_back(grad_mixed)
    grad_projected_low = grad_projected.astype(jnp.bfloat16)
    grad_out_weight = contract_rows(scaled_low, grad_projected_low)
    grad_scaled = contract_cols(grad_projected_low, full_out).reshape(heads_shape)
    grad_head_scale = jnp.sum(grad_scaled * context, axis=(0, 2))
    grad_context = (grad_scaled * head_scale[None, :, None]).astype(jnp.bfloat16)
    grad_queries, grad_keys, grad_values = attend_backward(
        queries, key_rows, value_rows, grad_context, log_totals, length, block_rows
    )
    grad_query_low = grad_queries.reshape(seq_len, width).astype(jnp.bfloat16)
    grad_key_low = grad_keys.reshape(seq_len, width).astype(jnp.bfloat16)
    grad_value_low = grad_values.reshape(seq_len, width).astype(jnp.bfloat16)
    grad_query_weight = contract_rows(normed_low, grad_query_low)
    grad_key_weight = contract_rows(normed_low, grad_key_low)
    grad_value_weight = contract_rows(normed_low, grad_value_low)
    grad_normed = (
        contract_cols(grad_query_low, full_query)
        + contract_cols(grad_key_low, full_key)
        + contract_cols(grad_value_low, full_value)
    )
    grad_inputs, grad_ln_gain, grad_ln_bias = first_back(grad_normed)
    grad_tokens = grad_mixed + grad_inputs
    grad_query_weight, grad_key_weight, grad_value_weight, grad_out_weight = (
        lax.psum_scatter(grad_query_weight, ("rows", "ffn"), scatter_dimension=0, tiled=True),
        lax.psum_scatter(grad_key_weight, ("rows", "ffn"), scatter_dimension=0, tiled=True),
        lax.psum_scatter(grad_value_weight, ("rows", "ffn"), scatter_dimension=0, tiled=True),
        lax.psum_scatter(grad_out_weight, ("rows", "ffn"), scatter_dimension=0, tiled=True),
    )
    small_sums = lax.psum(
        (
            grad_ln_gain,
            grad_ln_bias,
            jnp.sum(grad_query_low.astype(jnp.float32), axis=0),
            jnp.sum(grad_value_low.astype(jnp.float32), axis=0),
            grad_head_scale,
            jnp.sum(grad_projected_low.astype(jnp.float32), axis=0),
            grad_post_gain,
            grad_post_bias,
            grad_ffn_gain,
            grad_ffn_bias,
            jnp.sum(grad_result_low.astype(jnp.float32), axis=0),
        ),
        ("rows", "ffn"),
    )
    (
        grad_ln_gain,
        grad_ln_bias,
        grad_query_bias,
        grad_value_bias,
        grad_head_scale,
        grad_out_bias,
        grad_post_gain,
        grad_post_bias,
        grad_ffn_gain,
        grad_ffn_bias,
        grad_down_bias,
    ) = small_sums
    return (
        result,
        grad_tokens,
        grad_ln_gain,
        grad_ln_bias,
        grad_query_weight,
        grad_query_bias,
        grad_key_weight,
        grad_value_weight,
        grad_value_bias,
        grad_head_scale,
        grad_out_weight,
        grad_out_bias,
        grad_post_gain,
        grad_post_bias,
        grad_ffn_gain,
        grad_ffn_bias,
        grad_up,
        grad_up_bias,
        grad_mid_gain,
        grad_mid_bias,
        grad_down,
        grad_down_bias,
    )


def solution(mesh):
    placed = (
        P(("rows", "ffn"), None),
        P(("rows", "ffn")),
        P(("rows", "ffn"), None),
        P(),
        P(),
        P(("rows", "ffn"), None),
        P(),
        P(("rows", "ffn"), None),
        P(("rows", "ffn"), None),
        P(),
        P(),
        P(("rows", "ffn"), None),
        P(),
        P(),
        P(),
        P(),
        P(),
        P("rows", "ffn"),
        P(),
        P(),
        P(),
        P("rows", "ffn"),
        P(),
    )
    return jax.shard_map(
        shards,
        mesh=mesh,
        in_specs=placed,
        out_specs=(
            P(("rows", "ffn"), None),
            P(("rows", "ffn"), None),
            P(),
            P(),
            P(("rows", "ffn"), None),
            P(),
            P(("rows", "ffn"), None),
            P(("rows", "ffn"), None),
            P(),
            P(),
            P(("rows", "ffn"), None),
            P(),
            P(),
            P(),
            P(),
            P(),
            P("rows", "ffn"),
            P("ffn"),
            P("ffn"),
            P("ffn"),
            P("rows", "ffn"),
            P(),
        ),
        check_vma=False,
    )
```

profile of v0, /device:TPU:0, one launch (start us, length us, event | category | flops | bytes accessed | tf_op | source)
XLA Modules:
  0.0 1732.1 jit_solution(4929488624384349497)
XLA Ops:
  11.2 28.0 %all-gather.17.cloned.1.call-done = bf16[1024,512]{1,0:T(8,128)(2,1)} async-done(((bf16[256,512]{1,0:T(8,128)(2,1)}), bf16[1024,512]{1,0:T(8,128)(2,1)}) %all-gather.17.cloned.1.call-update) | async-done | bytes 1048592 | tf_op jit(solution)/shard_map/all_gather | solution.py:162
  43.8 3.9 copy.83
  49.9 17.8 %all-gather.21.cloned.1.call-done = bf16[1024,512]{1,0:T(8,128)(2,1)} async-done(((bf16[256,512]{1,0:T(8,128)(2,1)}), bf16[1024,512]{1,0:T(8,128)(2,1)}) %all-gather.21.cloned.1.call-update) | async-done | bytes 1048592 | tf_op jit(solution)/shard_map/all_gather | solution.py:163
  67.8 59.4 %all-gather.11.cloned.1.call-done = bf16[1024,1024]{1,0:T(8,128)(2,1)} async-done(((bf16[32,1024]{1,0:T(8,128)(2,1)}), bf16[1024,1024]{1,0:T(8,128)(2,1)}) %all-gather.11.cloned.1.call-update) | async-done | bytes 2097168 | tf_op jit(solution)/shard_map/all_gather | solution.py:139
  127.2 4.9 convolution_convert_fusion
  132.2 53.3 %all-gather.13.cloned.1.call-done = bf16[1024,1024]{1,0:T(8,128)(2,1)} async-done(((bf16[32,1024]{1,0:T(8,128)(2,1)}), bf16[1024,1024]{1,0:T(8,128)(2,1)}) %all-gather.13.cloned.1.call-update) | async-done | bytes 2097168 | tf_op jit(solution)/shard_map/all_gather | solution.py:140
  185.4 6.2 add_convert_fusion.4
  191.7 52.0 %all-gather.9.cloned.1.call-done = bf16[1024,1024]{1,0:T(8,128)(2,1)} async-done(((bf16[32,1024]{1,0:T(8,128)(2,1)}), bf16[1024,1024]{1,0:T(8,128)(2,1)}) %all-gather.9.cloned.1.call-update) | async-done | bytes 2097168 | tf_op jit(solution)/shard_map/all_gather | solution.py:138
  243.6 6.3 add_convert_fusion.5
  249.9 188.3 %while.27 = (s32[]{:T(128)}, f32[2,512,16,64]{1,0,3,2:T(2,128)}, f32[2,16,512]{2,1,0:T(8,128)S(1)}, s32[2]{0:T(128)S(1)}, s32[]{:T(128)}, /*index=5*/bf16[1024,1...) while((s32[]{:T(128)}, f32[2,512,16,64]{1,0,3,2:T(2,128)}, ...), condition=%wide.region_5.6_spmd, body=%wide.region_2.5_spmd.sunk | while | flops 2249188864 | bytes 127146176 | solution.py:61
  254.6 16.3 fusion.133
  271.0 15.1 fusion.134
  286.1 16.3 fusion.135
  302.4 3.5 copy.137
  305.9 38.2 %dynamic_update_slice.18 = f32[2,512,16,64]{1,0,3,2:T(2,128)} dynamic-update-slice(f32[2,512,16,64]{1,0,3,2:T(2,128)} %get-tuple-element.491, f32[1,512,16,64]{1,0,3,2:T(1,128)} %copy.137, s32[]{:T(128)} %get-tuple-element.490, s32[]{:T(128)} %constant.67.clone.1..sunk, s32[]{:T(128)} %constant.67.clone.1..sunk, s32[]{:T(128)} %constant.67.clone.1..sunk) | dynamic-update-slice | bytes 4194308 | tf_op jit(solution)/shard_map/while/body/jit(dynamic_update_index_in_dim)/dynamic_update_slice | solution.py:61
  348.3 16.3 fusion.133
  364.7 15.1 fusion.134
  379.8 16.5 fusion.135
  396.4 3.5 copy.137
  399.9 38.2 %dynamic_update_slice.18 = f32[2,512,16,64]{1,0,3,2:T(2,128)} dynamic-update-slice(f32[2,512,16,64]{1,0,3,2:T(2,128)} %get-tuple-element.491, f32[1,512,16,64]{1,0,3,2:T(1,128)} %copy.137, s32[]{:T(128)} %get-tuple-element.490, s32[]{:T(128)} %constant.67.clone.1..sunk, s32[]{:T(128)} %constant.67.clone.1..sunk, s32[]{:T(128)} %constant.67.clone.1..sunk) | dynamic-update-slice | bytes 4194308 | tf_op jit(solution)/shard_map/while/body/jit(dynamic_update_index_in_dim)/dynamic_update_slice | solution.py:61
  438.3 6.0 copy.134
  444.4 5.4 add_reduce_fusion
  458.9 51.2 %fusion.71 = (f32[1024]{0:T(1024)S(1)}, f32[1024]{0:T(1024)S(1)}, f32[1024,4096]{1,0:T(8,128)}, f32[1024,4096]{1,0:T(8,128)}, f32[1024,4096]{1,0:T(8,128)}) fusion(f32[4096]{0:T(1024)S(1)} %copy-done.52, bf16[1024,4096]{1,0:T(8,128)(2,1)} %all-gather.19.cloned.1.call-done, bf16[1024,1024]{0,1:T(8,128)(2,1)} %add_convert_fusion.7.clone.4), kind=kOutput, calls=%fused_computation.145 | convolution fusion | flops 8875145216 | bytes 60841984 | tf_op jit(solution)/shard_map/dot_general | solution.py:22
  510.2 22.7 %multiply_reduce_fusion.1 = (f32[4096]{0:T(1024)S(1)}, f32[1024]{0:T(1024)S(1)}, f32[1024]{0:T(1024)S(1)}, f32[4096]{0:T(1024)S(1)}, f32[1024,4096]{1,0:T(8,128)}) fusion(f32[1024,4096]{1,0:T(8,128)} %get-tuple-element.329, f32[1024]{0:T(1024)S(1)} %get-tuple-element.343, f32[1024]{0:T(1024)S(1)} %get-tuple-element.342, f32[4096]{0:T(1024)S(1)} %copy-done.53, ...), kind=kOutput, calls=%fused_computation.45 | convolution fusion | flops 8630818816 | bytes 44106752 | tf_op jit(solution)/shard_map/dot_general | solution.py:22
  532.9 30.2 %convert_reduce_fusion = (f32[4096]{0:T(1024)S(1)}, bf16[1024,4096]{1,0:T(8,128)(2,1)}, bf16[1024,4096]{1,0:T(8,128)(2,1)}) fusion(f32[1024,4096]{1,0:T(8,128)} %get-tuple-element.330, f32[1024]{0:T(1024)S(1)} %get-tuple-element.353, f32[1024]{0:T(1024)S(1)} %get-tuple-element.343, f32[1024,4096]{1,0:T(8,128)} %get-tuple-element.329, ...), kind=kLoop, calls=%fused_computation.46 | loop fusion | flops 113242112 | bytes 83968000 | tf_op jit(solution)/shard_map/reduce_sum | solution.py:191
  563.2 15.3 fusion.60
  578.6 14.4 fusion.47
  595.1 15.9 fusion.77
  611.1 5.4 copy.84
  616.4 4.3 multiply_reduce_fusion.9
  625.3 6.0 multiply_reduce_fusion.6
  631.4 114.3 %reduce-scatter.20.cloned.1.call-done = f32[1024,512]{1,0:T(8,128)} async-done(((f32[1024,4096]{1,0:T(8,128)}), f32[1024,512]{1,0:T(8,128)}) %reduce-scatter.20.cloned.1.call-update) | async-done | bytes 2097168 | tf_op jit(solution)/shard_map/reduce_scatter | solution.py:197
  748.5 4.2 fusion.73
  756.4 3.0 multiply_reduce_fusion.7
  761.4 153.2 %reduce-scatter.24.cloned.1.call-done = f32[1024,512]{1,0:T(8,128)} async-done(((f32[1024,4096]{1,0:T(8,128)}), f32[1024,512]{1,0:T(8,128)}) %reduce-scatter.24.cloned.1.call-update) | async-done | bytes 2097168 | tf_op jit(solution)/shard_map/reduce_scatter | solution.py:198
  917.4 229.4 %while.28 = (s32[]{:T(128)}, f32[1024,16,64]{0,2,1:T(8,128)}, f32[1024,16,64]{0,2,1:T(8,128)}, bf16[2,512,16,64]{1,3,2,0:T(8,128)(2,1)}, s32[2]{0:T(128)S(1)}, /...) while((s32[]{:T(128)}, f32[1024,16,64]{0,2,1:T(8,128)}, ...), condition=%wide.region_20.21_spmd.clone, body=%wide.region_18.20_spmd.clone.sunk | while | flops 5501347328 | bytes 375626592 | solution.py:98
  920.3 17.3 %fusion.145 = f32[16,512,1024]{2,1,0:T(8,128)} fusion(bf16[1024,16,64]{0,2,1:T(8,128)(2,1)S(1)} %get-tuple-element.547, bf16[1024,16,64]{0,2,1:T(8,128)(2,1)} %get-tuple-element.545, s32[]{:T(128)S(6)} %select_n.75), kind=kOutput, calls=%fused_computation.32.clone.1 | convolution fusion | flops 1073741824 | bytes 36700164 | tf_op jit(solution)/shard_map/while/body/eval_jaxpr/qhd,khd->hqk/dot_general | solution.py:41
  939.4 25.7 %multiply_reduce_fusion.13 = (f32[16,512]{1,0:T(8,128)S(1)}, f32[16,512,1024]{2,1,0:T(8,128)}) fusion(f32[16,512,1024]{2,1,0:T(8,128)} %fusion.145, f32[16,512]{1,0:T(8,128)S(1)} %dynamic-slice_bitcast_fusion.2, pred[512,1024]{1,0:T(8,128)(4,1)S(1)} %fusion.146, bf16[1024,16,64]{0,2,1:T(8,128)(2,1)S(1)} %copy-done.8, ...), kind=kOutput, calls=%fused_computation.18.clone.1 | convolution fusion | flops 1115676672 | bytes 70844416 | tf_op jit(solution)/shard_map/while/body/eval_jaxpr/qhd,khd->hqk/dot_general | solution.py:74
  965.2 28.2 %multiply_convert_fusion.6 = bf16[16,512,1024]{2,1,0:T(8,128)(2,1)} fusion(f32[16,512,1024]{2,1,0:T(8,128)} %get-tuple-element.477, f32[16,512,1024]{2,1,0:T(8,128)} %fusion.145, f32[16,512]{1,0:T(8,128)S(1)} %get-tuple-element.478, f32[16,512]{1,0:T(8,128)S(1)} %dynamic-slice_bitcast_fusion.2, pred[512,1024]{1,0:T(8,128)(4,1)S(1)} %fusion.146), kind=kLoop, calls=%fused_computation.17.clone.1 | loop fusion | flops 50331648 | bytes 84475904 | tf_op jit(solution)/shard_map/while/body/eval_jaxpr/convert_element_type | solution.py:84
  993.4 11.8 bitcast_add_fusion.4
  1006.0 7.8 bitcast_dynamic-update-slice_fusion.5
  1013.8 18.0 %bitcast_add_fusion.5 = f32[1024,16,64]{0,2,1:T(8,128)} fusion(f32[1024,16,64]{0,2,1:T(8,128)} %get-tuple-element.528, f32[16,512,1024]{2,1,0:T(8,128)} %fusion.145, f32[16,512]{1,0:T(8,128)S(1)} %dynamic-slice_bitcast_fusion.2, pred[512,1024]{1,0:T(8,128)(4,1)S(1)} %fusion.146, pred[]{:T(512)S(6)} %compare.3, ...), kind=kOutput, calls=%fused_computation.23.clone.1 | convolution fusion | flops 1109393408 | bytes 43548676 | tf_op jit(solution)/shard_map/while/body/eval_jaxpr/hqk,qhd->khd/dot_general | solution.py:77
  1034.4 17.0 fusion.145
  1053.2 25.6 %multiply_reduce_fusion.13 = (f32[16,512]{1,0:T(8,128)S(1)}, f32[16,512,1024]{2,1,0:T(8,128)}) fusion(f32[16,512,1024]{2,1,0:T(8,128)} %fusion.145, f32[16,512]{1,0:T(8,128)S(1)} %dynamic-slice_bitcast_fusion.2, pred[512,1024]{1,0:T(8,128)(4,1)S(1)} %fusion.146, bf16[1024,16,64]{0,2,1:T(8,128)(2,1)S(1)} %copy-done.8, ...), kind=kOutput, calls=%fused_computation.18.clone.1 | convolution fusion | flops 1115676672 | bytes 70844416 | tf_op jit(solution)/shard_map/while/body/eval_jaxpr/qhd,khd->hqk/dot_general | solution.py:74
  1078.8 27.8 %multiply_convert_fusion.6 = bf16[16,512,1024]{2,1,0:T(8,128)(2,1)} fusion(f32[16,512,1024]{2,1,0:T(8,128)} %get-tuple-element.477, f32[16,512,1024]{2,1,0:T(8,128)} %fusion.145, f32[16,512]{1,0:T(8,128)S(1)} %get-tuple-element.478, f32[16,512]{1,0:T(8,128)S(1)} %dynamic-slice_bitcast_fusion.2, pred[512,1024]{1,0:T(8,128)(4,1)S(1)} %fusion.146), kind=kLoop, calls=%fused_computation.17.clone.1 | loop fusion | flops 50331648 | bytes 84475904 | tf_op jit(solution)/shard_map/while/body/eval_jaxpr/convert_element_type | solution.py:84
  1106.5 12.5 bitcast_add_fusion.4
  1119.8 7.7 bitcast_dynamic-update-slice_fusion.5
  1127.5 19.1 %bitcast_add_fusion.5 = f32[1024,16,64]{0,2,1:T(8,128)} fusion(f32[1024,16,64]{0,2,1:T(8,128)} %get-tuple-element.528, f32[16,512,1024]{2,1,0:T(8,128)} %fusion.145, f32[16,512]{1,0:T(8,128)S(1)} %dynamic-slice_bitcast_fusion.2, pred[512,1024]{1,0:T(8,128)(4,1)S(1)} %fusion.146, pred[]{:T(512)S(6)} %compare.3, ...), kind=kOutput, calls=%fused_computation.23.clone.1 | convolution fusion | flops 1109393408 | bytes 43548676 | tf_op jit(solution)/shard_map/while/body/eval_jaxpr/hqk,qhd->khd/dot_general | solution.py:77
  1146.9 3.9 copy.85
  1152.7 4.5 fusion.66
  1161.0 4.4 fusion.62
  1169.5 4.3 fusion.64
  1174.5 7.2 fusion.57
  1183.9 4.7 fusion.78
  1196.4 3.3 add_add_fusion.3
  1199.6 5.4 copy.91
  1205.0 15.8 add_select_fusion
  1220.9 5.4 copy.90
  1226.5 39.9 %all-reduce = (f32[1024]{0:T(1024)}, f32[1024]{0:T(1024)}, f32[1024]{0:T(1024)}, f32[1024]{0:T(1024)}, f32[16]{0:T(128)}, /*index=5*/f32[1024]{0:T(1024)}, f32[1...) all-reduce(f32[1024]{0:T(1024)S(1)} %get-tuple-element.263, ...), channel_id=1, replica_groups=mesh['rows'=4,'ffn'=8] {'rows','ffn'}, use_global_device_ids=true, to_apply=%region_24.25 | all-reduce | flops 10256 | bytes 82048 | tf_op jit(solution)/shard_map/psum | solution.py:243
  1268.1 10.6 all-reduce.1
  1282.4 16.0 reduce-scatter.12.cloned.1.call-done
  1298.4 142.7 %reduce-scatter.16.cloned.1.call-done = f32[32,1024]{1,0:T(8,128)} async-done(((f32[1024,1024]{1,0:T(8,128)}), f32[32,1024]{1,0:T(8,128)}) %reduce-scatter.16.cloned.1.call-update) | async-done | bytes 131088 | tf_op jit(solution)/shard_map/reduce_scatter | solution.py:240
  1441.1 142.3 %reduce-scatter.14.cloned.1.call-done = f32[32,1024]{1,0:T(8,128)} async-done(((f32[1024,1024]{1,0:T(8,128)}), f32[32,1024]{1,0:T(8,128)}) %reduce-scatter.14.cloned.1.call-update) | async-done | bytes 131088 | tf_op jit(solution)/shard_map/reduce_scatter | solution.py:239
  1583.3 141.9 %reduce-scatter.18.cloned.1.call-done = f32[32,1024]{1,0:T(8,128)} async-done(((f32[1024,1024]{1,0:T(8,128)}), f32[32,1024]{1,0:T(8,128)}) %reduce-scatter.18.cloned.1.call-update) | async-done | bytes 131088 | tf_op jit(solution)/shard_map/reduce_scatter | solution.py:241
  (288 shorter events, 73.5 us)
Async XLA Ops:
  7.2 35.0 %copy-start.68 = (f32[16]{0:T(128)S(1)}, f32[16]{0:T(128)}, u32[]{:S(2)}) copy-start(f32[16]{0:T(128)} %param.37) | copy-start | bytes 196
  7.2 32.0 %all-gather.17.cloned.1.call-start = ((), (), s32[]{:S(2)}) async-start(), calls=%async_computation.13 | async-start | bytes 1310720 | tf_op jit(solution)/shard_map/all_gather | solution.py:162
  7.9 59.8 %all-gather.21.cloned.1.call-start = ((), (), s32[]{:S(2)}) async-start(), calls=%async_computation.15 | async-start | bytes 1310720 | tf_op jit(solution)/shard_map/all_gather | solution.py:163
  8.7 118.6 %all-gather.11.cloned.1.call-start = ((), (), s32[]{:S(2)}) async-start(), calls=%async_computation.10 | async-start | bytes 2162688 | tf_op jit(solution)/shard_map/all_gather | solution.py:139
  9.4 176.0 %all-gather.13.cloned.1.call-start = ((), (), s32[]{:S(2)}) async-start(), calls=%async_computation.11 | async-start | bytes 2162688 | tf_op jit(solution)/shard_map/all_gather | solution.py:140
  10.0 233.6 %all-gather.9.cloned.1.call-start = ((), (), s32[]{:S(2)}) async-start(), calls=%async_computation.9 | async-start | bytes 2162688 | tf_op jit(solution)/shard_map/all_gather | solution.py:138
  10.6 433.8 %all-gather.15.cloned.1.call-start = ((), (), s32[]{:S(2)}) async-start(), calls=%async_computation.12 | async-start | bytes 2162688 | tf_op jit(solution)/shard_map/all_gather | solution.py:141
  11.2 447.7 %all-gather.19.cloned.1.call-start = ((), (), s32[]{:S(2)}) async-start(), calls=%async_computation.14 | async-start | bytes 9437184 | tf_op jit(solution)/shard_map/all_gather | solution.py:166
  39.3 470.8 %all-gather.23.cloned.1.call-start = ((), (), s32[]{:S(2)}) async-start(), calls=%async_computation.16 | async-start | bytes 9437184 | tf_op jit(solution)/shard_map/all_gather | solution.py:167
  42.2 7.1 copy-start.9
  43.8 83.5 %copy-start.55 = (f32[1024]{0:T(1024)S(1)}, f32[1024]{0:T(1024)}, u32[]{:S(2)}) copy-start(f32[1024]{0:T(1024)} %param.30) | copy-start | bytes 12292
  43.8 83.5 %copy-start.77 = (f32[1024]{0:T(1024)S(1)}, f32[1024]{0:T(1024)}, u32[]{:S(2)}) copy-start(f32[1024]{0:T(1024)} %param.31) | copy-start | bytes 12292
  48.7 195.0 %copy-start.37 = (f32[1024]{0:T(1024)}, f32[1024]{0:T(1024)S(1)}, u32[]{:S(2)}) copy-start(f32[1024]{0:T(1024)S(1)} %broadcast_multiply_fusion.5) | copy-start | bytes 12292
  49.9 193.8 %copy-start.43 = (f32[1024]{0:T(1024)}, f32[1024]{0:T(1024)S(1)}, u32[]{:S(2)}) copy-start(f32[1024]{0:T(1024)S(1)} %fusion.52) | copy-start | bytes 12292
  67.8 117.7 %copy-start.75 = (f32[1024]{0:T(1024)S(1)}, f32[1024]{0:T(1024)}, u32[]{:S(2)}) copy-start(f32[1024]{0:T(1024)} %param.36) | copy-start | bytes 12292
  67.8 677.9 %reduce-scatter.20.cloned.1.call-start = ((), (), s32[]{:S(2)}) async-start(), calls=%async_computation.21 | async-start | bytes 18874368 | tf_op jit(solution)/shard_map/reduce_scatter | solution.py:197
  132.2 111.5 %copy-start.76 = (f32[1024]{0:T(1024)S(1)}, f32[1024]{0:T(1024)}, u32[]{:S(2)}) copy-start(f32[1024]{0:T(1024)} %param.33) | copy-start | bytes 12292
  271.0 15.1 copy-start.7
  364.7 15.2 copy-start.7
  438.2 6.1 copy-start.1
  438.2 6.1 copy-start.25
  438.2 6.1 copy-start.80
  438.3 6.1 copy-start.35
  438.3 6.1 copy-start.64
  458.9 51.2 %copy-start.17 = (bf16[1024,1024]{0,1:T(8,128)(2,1)S(1)}, bf16[1024,1024]{0,1:T(8,128)(2,1)}, u32[]{:S(2)}) copy-start(bf16[1024,1024]{0,1:T(8,128)(2,1)} %copy.83) | copy-start | bytes 6291460
  458.9 51.2 %copy-start.53 = (f32[4096]{0:T(1024)S(1)}, f32[4096]{0:T(1024)}, u32[]{:S(2)}) copy-start(f32[4096]{0:T(1024)} %param.46) | copy-start | bytes 49156
  458.9 51.2 %copy-start.70 = (pred[1024]{0:T(1024)(128)(4,1)S(1)}, pred[1024]{0:T(1024)(128)(4,1)}, u32[]{:S(2)}) copy-start(pred[1024]{0:T(1024)(128)(4,1)} %iota_compare_fusion.4) | copy-start | bytes 3076
  510.1 22.7 %copy-start.54 = (f32[4096]{0:T(1024)S(1)}, f32[4096]{0:T(1024)}, u32[]{:S(2)}) copy-start(f32[4096]{0:T(1024)} %param.47) | copy-start | bytes 49156
  532.9 30.3 %copy-start.5 = (f32[1024,1024]{0,1:T(8,128)S(1)}, f32[1024,1024]{0,1:T(8,128)}, u32[]{:S(2)}) copy-start(f32[1024,1024]{0,1:T(8,128)} %copy-done.4) | copy-start | bytes 12582916
  532.9 30.3 %copy-start.28 = (f32[1024]{0:T(1024)S(1)}, f32[1024]{0:T(1024)}, u32[]{:S(2)}) copy-start(f32[1024]{0:T(1024)} %copy-done.27) | copy-start | bytes 12292
  532.9 30.3 %copy-start.32 = (f32[1024]{0:T(1024)S(1)}, f32[1024]{0:T(1024)}, u32[]{:S(2)}) copy-start(f32[1024]{0:T(1024)} %param.42) | copy-start | bytes 12292
  532.9 30.3 %copy-start.34 = (f32[1024]{0:T(1024)S(1)}, f32[1024]{0:T(1024)}, u32[]{:S(2)}) copy-start(f32[1024]{0:T(1024)} %copy-done.33) | copy-start | bytes 12292
  532.9 30.3 %copy-start.63 = (f32[1024]{0:T(1024)S(1)}, f32[1024]{0:T(1024)}, u32[]{:S(2)}) copy-start(f32[1024]{0:T(1024)} %param.43) | copy-start | bytes 12292
  578.6 336.0 %reduce-scatter.24.cloned.1.call-start = ((), (), s32[]{:S(2)}) async-start(), calls=%async_computation.23 | async-start | bytes 18874368 | tf_op jit(solution)/shard_map/reduce_scatter | solution.py:198
  593.0 673.3 %reduce-scatter.28.cloned.1.call-start = ((), (), s32[]{:S(2)}) async-start(), calls=%async_computation.25 | async-start | bytes 2359296
  616.4 6.1 copy-start.14
  625.3 6.1 copy-start.48
  631.3 647.4 %reduce-scatter.22.cloned.1.call-start = ((), (), s32[]{:S(2)}) async-start(), calls=%async_computation.22 | async-start | bytes 1310720 | tf_op jit(solution)/shard_map/reduce_scatter | solution.py:202
  748.4 532.1 %reduce-scatter.26.cloned.1.call-start = ((), (), s32[]{:S(2)}) async-start(), calls=%async_computation.24 | async-start | bytes 1310720 | tf_op jit(solution)/shard_map/reduce_scatter | solution.py:205
  753.7 5.7 copy-start.21
  759.4 158.0 %copy-start.2 = (bf16[1024,16,64]{0,2,1:T(8,128)(2,1)S(1)}, bf16[1024,16,64]{0,2,1:T(8,128)(2,1)}, u32[]{:S(2)}) copy-start(bf16[1024,16,64]{0,2,1:T(8,128)(2,1)} %copy-done.1) | copy-start | bytes 6291460
  759.4 158.0 %copy-start.26 = (f32[2,16,512]{2,1,0:T(8,128)S(1)}, f32[2,16,512]{2,1,0:T(8,128)}, u32[]{:S(2)}) copy-start(f32[2,16,512]{2,1,0:T(8,128)} %copy-done.25) | copy-start | bytes 196612
  759.4 158.0 %copy-start.81 = (s32[2]{0:T(128)S(1)}, s32[2]{0:T(128)}, u32[]{:S(2)}) copy-start(s32[2]{0:T(128)} %copy-done.80) | copy-start | bytes 28
  917.3 381.1 %reduce-scatter.12.cloned.1.call-start = ((), (), s32[]{:S(2)}) async-start(), calls=%async_computation.17 | async-start | bytes 4325376 | tf_op jit(solution)/shard_map/reduce_scatter | solution.py:238
  920.3 19.1 %copy-start.8 = (bf16[1024,16,64]{0,2,1:T(8,128)(2,1)S(1)}, bf16[1024,16,64]{0,2,1:T(8,128)(2,1)}, u32[]{:S(2)}) copy-start(bf16[1024,16,64]{0,2,1:T(8,128)(2,1)} %get-tuple-element.550) | copy-start | bytes 6291460 | tf_op jit(solution)/shard_map/while
  920.3 19.1 %copy-start.16 = (bf16[1024,16,64]{0,2,1:T(8,128)(2,1)S(1)}, bf16[1024,16,64]{0,2,1:T(8,128)(2,1)}, u32[]{:S(2)}) copy-start(bf16[1024,16,64]{0,2,1:T(8,128)(2,1)} %get-tuple-element.549) | copy-start | bytes 6291460 | tf_op jit(solution)/shard_map/while
  993.4 12.6 copy-start
  1013.8 18.0 %copy-start.3 = (bf16[1024,16,64]{0,2,1:T(8,128)(2,1)S(1)}, bf16[1024,16,64]{0,2,1:T(8,128)(2,1)}, u32[]{:S(2)}) copy-start(bf16[1024,16,64]{0,2,1:T(8,128)(2,1)} %get-tuple-element.586) | copy-start | bytes 6291460 | tf_op jit(solution)/shard_map/while
  1034.4 18.8 %copy-start.8 = (bf16[1024,16,64]{0,2,1:T(8,128)(2,1)S(1)}, bf16[1024,16,64]{0,2,1:T(8,128)(2,1)}, u32[]{:S(2)}) copy-start(bf16[1024,16,64]{0,2,1:T(8,128)(2,1)} %get-tuple-element.550) | copy-start | bytes 6291460 | tf_op jit(solution)/shard_map/while
  1034.4 18.8 %copy-start.16 = (bf16[1024,16,64]{0,2,1:T(8,128)(2,1)S(1)}, bf16[1024,16,64]{0,2,1:T(8,128)(2,1)}, u32[]{:S(2)}) copy-start(bf16[1024,16,64]{0,2,1:T(8,128)(2,1)} %get-tuple-element.549) | copy-start | bytes 6291460 | tf_op jit(solution)/shard_map/while
  1106.5 13.3 copy-start
  1127.5 19.1 %copy-start.3 = (bf16[1024,16,64]{0,2,1:T(8,128)(2,1)S(1)}, bf16[1024,16,64]{0,2,1:T(8,128)(2,1)}, u32[]{:S(2)}) copy-start(bf16[1024,16,64]{0,2,1:T(8,128)(2,1)} %get-tuple-element.586) | copy-start | bytes 6291460 | tf_op jit(solution)/shard_map/while
  1146.8 5.8 copy-start.11
  1146.8 5.8 copy-start.38
  1146.8 5.8 copy-start.44
  1146.8 5.8 copy-start.56
  1146.8 5.8 copy-start.78
  1157.2 283.9 %reduce-scatter.16.cloned.1.call-start = ((), (), s32[]{:S(2)}) async-start(), calls=%async_computation.19 | async-start | bytes 4325376 | tf_op jit(solution)/shard_map/reduce_scatter | solution.py:240
  1165.5 417.8 %reduce-scatter.14.cloned.1.call-start = ((), (), s32[]{:S(2)}) async-start(), calls=%async_computation.18 | async-start | bytes 4325376 | tf_op jit(solution)/shard_map/reduce_scatter | solution.py:239
  1173.8 551.4 %reduce-scatter.18.cloned.1.call-start = ((), (), s32[]{:S(2)}) async-start(), calls=%async_computation.20 | async-start | bytes 4325376 | tf_op jit(solution)/shard_map/reduce_scatter | solution.py:241
  1220.8 5.6 copy-start.58
  1220.8 5.6 copy-start.59
  1220.8 5.6 copy-start.60
  1220.9 5.6 copy-start.67
  (40 other events, 120.2 us)
Sparse Core Ops, SparseCore 0:
  9.9 29.3 all-gather.16
  41.1 26.6 all-gather.20
  70.7 56.4 all-gather.10
  130.1 55.3 all-gather.12
  188.3 55.3 all-gather.8
  246.5 55.3 all-gather.14
  303.5 81.0 all-gather.18
  386.2 80.4 all-gather.22
  578.7 166.9 reduce-scatter.19
  747.9 166.6 reduce-scatter.23
  916.8 34.1 reduce-scatter.27
  953.8 26.1 reduce-scatter.21
  983.1 27.7 reduce-scatter.25
  1157.3 141.0 reduce-scatter.11
  1301.1 139.9 reduce-scatter.15
  1443.8 139.5 reduce-scatter.13
  1586.0 139.1 reduce-scatter.17
where the time goes:
time: 1750 us; the launch traced here: 1730 us
  waiting for transfers between devices  925 us (53%)
  matrix products  420 us (24%)
  other arithmetic  171 us (10%)
  local copies, waits for them, and re-layouts  140 us (8%)
  blocking collectives  50.5 us (3%)
    reduce_scatter x1, waiting for transfers between devices, shards(): lax.psum_scatter(grad_down_full, 'ffn', scatter_dimension=1, tiled=True)  153 us
    reduce_scatter x1, waiting for transfers between devices, shards(): lax.psum_scatter(grad_value_weight, ('rows', 'ffn'), scatter_dimension=0,...  143 us
    reduce_scatter x1, waiting for transfers between devices, shards(): lax.psum_scatter(grad_key_weight, ('rows', 'ffn'), scatter_dimension=0, t...  142 us
    reduce_scatter x1, waiting for transfers between devices, shards(): lax.psum_scatter(grad_out_weight, ('rows', 'ffn'), scatter_dimension=0, t...  142 us
    reduce_scatter x1, waiting for transfers between devices, shards(): lax.psum_scatter(grad_up_full, 'ffn', scatter_dimension=1, tiled=True)  114 us
    dot_general x6, matrix products, plain_dot(): return jnp.dot(left, right, preferred_element_type=jnp.float32)  96.6 us
    dynamic_update_slice x4, local copies, waits for them, and re-layouts, attend_forward(): context, log_totals = lax.map(one_block, firsts)  83.4 us
    dot_general x4, matrix products, block_scores(): jnp.einsum('qhd,khd->hqk', rows_here, key_rows, preferred_element_type=jn...  67 us
  transfers between devices with their start and end apart: 17, of which 11 were waited for; matrix products, arithmetic and copies ran while one was open for 37% of the time, Pallas kernels for 0%

commit v1 on v0

--- a/solution.py
+++ b/solution.py
@@ -5,6 +5,18 @@
 
 epsilon = 1e-05
 masked_score = -1e30
+
+
+def gather_by_bits(shard, axis, dim):
+    ways, here, step = (lax.axis_size(axis), lax.axis_index(axis), shard.shape[dim])
+    line, have = (shard, 1)
+    while have < ways:
+        line = jnp.concatenate(
+            [line, lax.ppermute(line, axis, [(d, (d - have) % ways) for d in range(ways)])],
+            axis=dim,
+        )
+        have = 2 * have
+    return jnp.roll(line, here * step, axis=dim)
 
 
 def layer_norm(values, gain, shift):
@@ -136,7 +148,7 @@
     inputs = tokens.astype(jnp.float32)
     full_query, full_key, full_value, full_out = (
         lax.all_gather(w_query, ("rows", "ffn"), axis=0, tiled=True),
-        lax.all_gather(w_key, ("rows", "ffn"), axis=0, tiled=True),
+        gather_by_bits(w_key, ("rows", "ffn"), 0),
         lax.all_gather(w_value, ("rows", "ffn"), axis=0, tiled=True),
         lax.all_gather(w_out, ("rows", "ffn"), axis=0, tiled=True),
     )

time: 1750 us -> 1570 us (0.90)
  waiting for transfers between devices: 925 us -> 720 us
    reduce_scatter x1, waiting for transfers between devices: 142 us -> 0.01 us  [shards(): lax.psum_scatter(grad_out_weight, ('rows', 'ffn'), scatter_dimension=0, t...]
    all_gather x1 -> x0, waiting for transfers between devices: 59.4 us -> none  [shards(): lax.all_gather(w_key, ('rows', 'ffn'), axis=0, tiled=True)]
    ppermute x0 -> x5, waiting for transfers between devices: none -> 43.5 us  [gather_by_bits(): lax.ppermute(line, axis, [(d, (d - have) % ways) for d in range(ways)])]
    all_gather x1, waiting for transfers between devices: 53.3 us -> 11.4 us  [shards(): lax.all_gather(w_value, ('rows', 'ffn'), axis=0, tiled=True)]
    all_gather x1, waiting for transfers between devices: 17.8 us -> 0.02 us  [shards(): lax.all_gather(w_down, 'rows', axis=0, tiled=True)]
    unnamed x164 -> x176, local copies, waits for them, and re-layouts: 40.8 us -> 52.9 us
  transfers between devices with their start and end apart: 17 -> 21, of which waited for: 11 -> 13; matrix products, arithmetic and copies ran while one was open for 37% -> 43% of each run, Pallas kernels for 0% -> 0%
where the time goes in v1:
time: 1570 us; the launch traced here: 1550 us
  waiting for transfers between devices  720 us (46%)
  matrix products  417 us (27%)
  other arithmetic  180 us (11%)
  local copies, waits for them, and re-layouts  154 us (10%)
  blocking collectives  50.5 us (3%)
  between operations  15.9 us (1%)
    reduce_scatter x1, waiting for transfers between devices, shards(): lax.psum_scatter(grad_down_full, 'ffn', scatter_dimension=1, tiled=True)  148 us
    reduce_scatter x1, waiting for transfers between devices, shards(): lax.psum_scatter(grad_value_weight, ('rows', 'ffn'), scatter_dimension=0,...  142 us
    reduce_scatter x1, waiting for transfers between devices, shards(): lax.psum_scatter(grad_key_weight, ('rows', 'ffn'), scatter_dimension=0, t...  142 us
    reduce_scatter x1, waiting for transfers between devices, shards(): lax.psum_scatter(grad_up_full, 'ffn', scatter_dimension=1, tiled=True)  125 us
    dot_general x6, matrix products, plain_dot(): return jnp.dot(left, right, preferred_element_type=jnp.float32)  96.3 us
    dynamic_update_slice x4, local copies, waits for them, and re-layouts, attend_forward(): context, log_totals = lax.map(one_block, firsts)  83.4 us
    dot_general x4, matrix products, block_scores(): jnp.einsum('qhd,khd->hqk', rows_here, key_rows, preferred_element_type=jn...  66.9 us
    convert_element_type x2, other arithmetic, one_block(): grad_scores = (probs * (grad_probs - inner)).astype(jnp.bfloat16)  56.5 us
  transfers between devices with their start and end apart: 21, of which 13 were waited for; matrix products, arithmetic and copies ran while one was open for 43% of the time, Pallas kernels for 0%

profile of v1, /device:TPU:0, one launch (start us, length us, event | category | flops | bytes accessed | tf_op | source)
XLA Modules:
  0.0 1554.6 jit_solution(10046734970111701029)
XLA Ops:
  10.6 28.6 %all-gather.14.cloned.1.call-done = bf16[1024,512]{1,0:T(8,128)(2,1)} async-done(((bf16[256,512]{1,0:T(8,128)(2,1)}), bf16[1024,512]{1,0:T(8,128)(2,1)}) %all-gather.14.cloned.1.call-update) | async-done | bytes 1048592 | tf_op jit(solution)/shard_map/all_gather | solution.py:174
  39.3 3.7 collective-permute-start
  46.7 4.4 collective-permute-done.1
  52.1 15.0 collective-permute-done.2
  73.5 8.5 collective-permute-done.3
  89.5 3.9 copy.83
  95.8 13.4 collective-permute-done.4
  117.4 4.6 convolution_convert_fusion
  122.0 11.4 all-gather.10.cloned.1.call-done
  133.4 6.3 add_convert_fusion.4
  139.6 51.9 %all-gather.8.cloned.1.call-done = bf16[1024,1024]{1,0:T(8,128)(2,1)} async-done(((bf16[32,1024]{1,0:T(8,128)(2,1)}), bf16[1024,1024]{1,0:T(8,128)(2,1)}) %all-gather.8.cloned.1.call-update) | async-done | bytes 2097168 | tf_op jit(solution)/shard_map/all_gather | solution.py:150
  191.6 6.3 add_convert_fusion.5
  197.9 189.6 %while.27 = (s32[]{:T(128)}, f32[2,512,16,64]{1,0,3,2:T(2,128)}, f32[2,16,512]{2,1,0:T(8,128)}, s32[2]{0:T(128)S(1)}, s32[]{:T(128)}, /*index=5*/bf16[1024,16,64...) while((s32[]{:T(128)}, f32[2,512,16,64]{1,0,3,2:T(2,128)}, ...), condition=%wide.region_5.6_spmd, body=%wide.region_2.5_spmd.sunk | while | flops 2249188864 | bytes 127146688 | solution.py:73
  202.6 16.3 %fusion.135 = (f32[16,512]{1,0:T(8,128)S(1)}, f32[16,512,1024]{2,1,0:T(8,128)}) fusion(pred[512,1024]{1,0:T(8,128)(4,1)S(1)} %fusion.134, bf16[1024,16,64]{0,2,1:T(8,128)(2,1)S(1)} %get-tuple-element.517, bf16[1024,16,64]{0,2,1:T(8,128)(2,1)} %get-tuple-element.516, s32[]{:T(128)S(6)} %select_n.86), kind=kOutput, calls=%fused_computation.3.clone.1 | convolution fusion | flops 1098899456 | bytes 37257220 | tf_op jit(solution)/shard_map/while/body/eval_jaxpr/qhd,khd->hqk/dot_general | solution.py:53
  218.9 15.1 fusion.136
  234.6 16.1 %fusion.137 = f32[1,512,16,64]{1,3,2,0:T(8,128)S(1)} fusion(bf16[1024,16,64]{0,2,1:T(8,128)(2,1)S(1)} %copy-done.7, f32[16,512,1024]{2,1,0:T(8,128)} %get-tuple-element.474, f32[16,512]{1,0:T(8,128)S(1)} %fusion.136, f32[16,512]{1,0:T(8,128)S(1)} %get-tuple-element.475, pred[512,1024]{1,0:T(8,128)(4,1)S(1)} %fusion.134), kind=kOutput, calls=%fused_computation.8.clone.1 | convolution fusion | flops 1115684864 | bytes 38338560 | tf_op jit(solution)/shard_map/while/body/eval_jaxpr/hqk,khd->qhd/dot_general | solution.py:69
  250.7 3.5 copy.137
  254.2 38.2 %dynamic_update_slice.18 = f32[2,512,16,64]{1,0,3,2:T(2,128)} dynamic-update-slice(f32[2,512,16,64]{1,0,3,2:T(2,128)} %get-tuple-element.501, f32[1,512,16,64]{1,0,3,2:T(1,128)} %copy.137, s32[]{:T(128)} %get-tuple-element.500, s32[]{:T(128)} %constant.74.clone.1..sunk, s32[]{:T(128)} %constant.74.clone.1..sunk, s32[]{:T(128)} %constant.74.clone.1..sunk) | dynamic-update-slice | bytes 4194308 | tf_op jit(solution)/shard_map/while/body/jit(dynamic_update_index_in_dim)/dynamic_update_slice | solution.py:73
  296.7 16.3 %fusion.135 = (f32[16,512]{1,0:T(8,128)S(1)}, f32[16,512,1024]{2,1,0:T(8,128)}) fusion(pred[512,1024]{1,0:T(8,128)(4,1)S(1)} %fusion.134, bf16[1024,16,64]{0,2,1:T(8,128)(2,1)S(1)} %get-tuple-element.517, bf16[1024,16,64]{0,2,1:T(8,128)(2,1)} %get-tuple-element.516, s32[]{:T(128)S(6)} %select_n.86), kind=kOutput, calls=%fused_computation.3.clone.1 | convolution fusion | flops 1098899456 | bytes 37257220 | tf_op jit(solution)/shard_map/while/body/eval_jaxpr/qhd,khd->hqk/dot_general | solution.py:53
  313.0 15.2 fusion.136
  328.8 16.8 %fusion.137 = f32[1,512,16,64]{1,3,2,0:T(8,128)S(1)} fusion(bf16[1024,16,64]{0,2,1:T(8,128)(2,1)S(1)} %copy-done.7, f32[16,512,1024]{2,1,0:T(8,128)} %get-tuple-element.474, f32[16,512]{1,0:T(8,128)S(1)} %fusion.136, f32[16,512]{1,0:T(8,128)S(1)} %get-tuple-element.475, pred[512,1024]{1,0:T(8,128)(4,1)S(1)} %fusion.134), kind=kOutput, calls=%fused_computation.8.clone.1 | convolution fusion | flops 1115684864 | bytes 38338560 | tf_op jit(solution)/shard_map/while/body/eval_jaxpr/hqk,khd->qhd/dot_general | solution.py:69
  345.6 3.5 copy.137
  349.1 38.2 %dynamic_update_slice.18 = f32[2,512,16,64]{1,0,3,2:T(2,128)} dynamic-update-slice(f32[2,512,16,64]{1,0,3,2:T(2,128)} %get-tuple-element.501, f32[1,512,16,64]{1,0,3,2:T(1,128)} %copy.137, s32[]{:T(128)} %get-tuple-element.500, s32[]{:T(128)} %constant.74.clone.1..sunk, s32[]{:T(128)} %constant.74.clone.1..sunk, s32[]{:T(128)} %constant.74.clone.1..sunk) | dynamic-update-slice | bytes 4194308 | tf_op jit(solution)/shard_map/while/body/jit(dynamic_update_index_in_dim)/dynamic_update_slice | solution.py:73
  387.5 6.0 copy.134
  393.5 5.3 add_reduce_fusion
  408.0 51.2 %fusion.75 = (f32[1024]{0:T(1024)S(1)}, f32[1024]{0:T(1024)S(1)}, f32[1024,4096]{1,0:T(8,128)}, f32[1024,4096]{1,0:T(8,128)}, f32[1024,4096]{1,0:T(8,128)}) fusion(f32[4096]{0:T(1024)S(1)} %copy-done.53, bf16[1024,4096]{1,0:T(8,128)(2,1)} %all-gather.16.cloned.1.call-done, bf16[1024,1024]{0,1:T(8,128)(2,1)} %add_convert_fusion.7.clone.4), kind=kOutput, calls=%fused_computation.169 | convolution fusion | flops 8875145216 | bytes 60841984 | tf_op jit(solution)/shard_map/dot_general | solution.py:34
  459.3 22.6 %multiply_reduce_fusion.1 = (f32[4096]{0:T(1024)S(1)}, f32[1024]{0:T(1024)S(1)}, f32[1024]{0:T(1024)S(1)}, f32[4096]{0:T(1024)S(1)}, f32[1024,4096]{1,0:T(8,128)}) fusion(f32[1024,4096]{1,0:T(8,128)} %get-tuple-element.329, f32[1024]{0:T(1024)S(1)} %get-tuple-element.353, f32[1024]{0:T(1024)S(1)} %get-tuple-element.352, f32[4096]{0:T(1024)S(1)} %copy-done.54, ...), kind=kOutput, calls=%fused_computation.45 | convolution fusion | flops 8630818816 | bytes 44106752 | tf_op jit(solution)/shard_map/dot_general | solution.py:34
  482.0 30.2 %convert_reduce_fusion = (f32[4096]{0:T(1024)S(1)}, bf16[1024,4096]{1,0:T(8,128)(2,1)}, bf16[1024,4096]{1,0:T(8,128)(2,1)}) fusion(f32[1024,4096]{1,0:T(8,128)} %get-tuple-element.330, f32[1024]{0:T(1024)S(1)} %get-tuple-element.363, f32[1024]{0:T(1024)S(1)} %get-tuple-element.353, f32[1024,4096]{1,0:T(8,128)} %get-tuple-element.329, ...), kind=kLoop, calls=%fused_computation.46 | loop fusion | flops 113242112 | bytes 83968000 | tf_op jit(solution)/shard_map/reduce_sum | solution.py:203
  512.3 15.3 fusion.64
  527.6 14.4 fusion.49
  544.2 15.8 %fusion.81 = (f32[1024]{0:T(1024)}, f32[1024,1024]{1,0:T(8,128)}) fusion(bf16[1024,4096]{1,0:T(8,128)(2,1)} %get-tuple-element.321, bf16[1024,4096]{1,0:T(8,128)(2,1)} %all-gather.16.cloned.1.call-done), kind=kOutput, calls=%fused_computation.174 | convolution fusion | flops 8590982144 | bytes 20975616 | tf_op jit(solution)/shard_map/dot_general | solution.py:44
  560.0 5.4 copy.84
  565.4 4.1 multiply_reduce_fusion.9
  569.7 125.2 %reduce-scatter.20.cloned.1.call-done = f32[1024,512]{1,0:T(8,128)} async-done(((f32[1024,4096]{1,0:T(8,128)}), f32[1024,512]{1,0:T(8,128)}) %reduce-scatter.20.cloned.1.call-update) | async-done | bytes 2097168 | tf_op jit(solution)/shard_map/reduce_scatter | solution.py:209
  697.7 5.4 multiply_reduce_fusion.5
  704.4 6.5 multiply_reduce_fusion.6
  715.7 148.2 %reduce-scatter.24.cloned.1.call-done = f32[1024,512]{1,0:T(8,128)} async-done(((f32[1024,4096]{1,0:T(8,128)}), f32[1024,512]{1,0:T(8,128)}) %reduce-scatter.24.cloned.1.call-update) | async-done | bytes 2097168 | tf_op jit(solution)/shard_map/reduce_scatter | solution.py:210
  875.8 4.4 fusion.61
  881.8 230.1 %while.28 = (s32[]{:T(128)}, f32[1024,16,64]{0,2,1:T(8,128)}, f32[1024,16,64]{0,2,1:T(8,128)}, bf16[2,512,16,64]{1,3,2,0:T(8,128)(2,1)}, s32[2]{0:T(128)S(1)}, /...) while((s32[]{:T(128)}, f32[1024,16,64]{0,2,1:T(8,128)}, ...), condition=%wide.region_20.21_spmd.clone, body=%wide.region_18.20_spmd.clone.sunk | while | flops 5501347328 | bytes 375626592 | solution.py:110
  884.7 17.2 %fusion.147 = f32[16,512,1024]{2,1,0:T(8,128)} fusion(bf16[1024,16,64]{0,2,1:T(8,128)(2,1)S(1)} %get-tuple-element.557, bf16[1024,16,64]{0,2,1:T(8,128)(2,1)} %get-tuple-element.555, s32[]{:T(128)S(6)} %select_n.90), kind=kOutput, calls=%fused_computation.32.clone.1 | convolution fusion | flops 1073741824 | bytes 36700164 | tf_op jit(solution)/shard_map/while/body/eval_jaxpr/qhd,khd->hqk/dot_general | solution.py:53
  903.7 25.8 %multiply_reduce_fusion.13 = (f32[16,512]{1,0:T(8,128)S(1)}, f32[16,512,1024]{2,1,0:T(8,128)}) fusion(f32[16,512,1024]{2,1,0:T(8,128)} %fusion.147, f32[16,512]{1,0:T(8,128)S(1)} %dynamic-slice_bitcast_fusion.2, pred[512,1024]{1,0:T(8,128)(4,1)S(1)} %fusion.148, bf16[1024,16,64]{0,2,1:T(8,128)(2,1)S(1)} %copy-done.8, ...), kind=kOutput, calls=%fused_computation.18.clone.1 | convolution fusion | flops 1115676672 | bytes 70844416 | tf_op jit(solution)/shard_map/while/body/eval_jaxpr/qhd,khd->hqk/dot_general | solution.py:86
  929.5 28.3 %multiply_convert_fusion.6 = bf16[16,512,1024]{2,1,0:T(8,128)(2,1)} fusion(f32[16,512,1024]{2,1,0:T(8,128)} %get-tuple-element.487, f32[16,512,1024]{2,1,0:T(8,128)} %fusion.147, f32[16,512]{1,0:T(8,128)S(1)} %get-tuple-element.488, f32[16,512]{1,0:T(8,128)S(1)} %dynamic-slice_bitcast_fusion.2, pred[512,1024]{1,0:T(8,128)(4,1)S(1)} %fusion.148), kind=kLoop, calls=%fused_computation.17.clone.1 | loop fusion | flops 50331648 | bytes 84475904 | tf_op jit(solution)/shard_map/while/body/eval_jaxpr/convert_element_type | solution.py:96
  957.9 11.5 bitcast_add_fusion.4
  970.2 7.8 bitcast_dynamic-update-slice_fusion.5
  977.9 18.1 %bitcast_add_fusion.5 = f32[1024,16,64]{0,2,1:T(8,128)} fusion(f32[1024,16,64]{0,2,1:T(8,128)} %get-tuple-element.538, f32[16,512,1024]{2,1,0:T(8,128)} %fusion.147, f32[16,512]{1,0:T(8,128)S(1)} %dynamic-slice_bitcast_fusion.2, pred[512,1024]{1,0:T(8,128)(4,1)S(1)} %fusion.148, pred[]{:T(512)S(6)} %compare.4, ...), kind=kOutput, calls=%fused_computation.23.clone.1 | convolution fusion | flops 1109393408 | bytes 43548676 | tf_op jit(solution)/shard_map/while/body/eval_jaxpr/hqk,qhd->khd/dot_general | solution.py:89
  998.5 17.1 %fusion.147 = f32[16,512,1024]{2,1,0:T(8,128)} fusion(bf16[1024,16,64]{0,2,1:T(8,128)(2,1)S(1)} %get-tuple-element.557, bf16[1024,16,64]{0,2,1:T(8,128)(2,1)} %get-tuple-element.555, s32[]{:T(128)S(6)} %select_n.90), kind=kOutput, calls=%fused_computation.32.clone.1 | convolution fusion | flops 1073741824 | bytes 36700164 | tf_op jit(solution)/shard_map/while/body/eval_jaxpr/qhd,khd->hqk/dot_general | solution.py:53
  1017.4 25.7 %multiply_reduce_fusion.13 = (f32[16,512]{1,0:T(8,128)S(1)}, f32[16,512,1024]{2,1,0:T(8,128)}) fusion(f32[16,512,1024]{2,1,0:T(8,128)} %fusion.147, f32[16,512]{1,0:T(8,128)S(1)} %dynamic-slice_bitcast_fusion.2, pred[512,1024]{1,0:T(8,128)(4,1)S(1)} %fusion.148, bf16[1024,16,64]{0,2,1:T(8,128)(2,1)S(1)} %copy-done.8, ...), kind=kOutput, calls=%fused_computation.18.clone.1 | convolution fusion | flops 1115676672 | bytes 70844416 | tf_op jit(solution)/shard_map/while/body/eval_jaxpr/qhd,khd->hqk/dot_general | solution.py:86
  1043.1 28.1 %multiply_convert_fusion.6 = bf16[16,512,1024]{2,1,0:T(8,128)(2,1)} fusion(f32[16,512,1024]{2,1,0:T(8,128)} %get-tuple-element.487, f32[16,512,1024]{2,1,0:T(8,128)} %fusion.147, f32[16,512]{1,0:T(8,128)S(1)} %get-tuple-element.488, f32[16,512]{1,0:T(8,128)S(1)} %dynamic-slice_bitcast_fusion.2, pred[512,1024]{1,0:T(8,128)(4,1)S(1)} %fusion.148), kind=kLoop, calls=%fused_computation.17.clone.1 | loop fusion | flops 50331648 | bytes 84475904 | tf_op jit(solution)/shard_map/while/body/eval_jaxpr/convert_element_type | solution.py:96
  1071.2 12.7 bitcast_add_fusion.4
  1084.9 7.7 bitcast_dynamic-update-slice_fusion.5
  1092.6 19.2 %bitcast_add_fusion.5 = f32[1024,16,64]{0,2,1:T(8,128)} fusion(f32[1024,16,64]{0,2,1:T(8,128)} %get-tuple-element.538, f32[16,512,1024]{2,1,0:T(8,128)} %fusion.147, f32[16,512]{1,0:T(8,128)S(1)} %dynamic-slice_bitcast_fusion.2, pred[512,1024]{1,0:T(8,128)(4,1)S(1)} %fusion.148, pred[]{:T(512)S(6)} %compare.4, ...), kind=kOutput, calls=%fused_computation.23.clone.1 | convolution fusion | flops 1109393408 | bytes 43548676 | tf_op jit(solution)/shard_map/while/body/eval_jaxpr/hqk,qhd->khd/dot_general | solution.py:89
  1112.0 3.9 copy.85
  1117.8 4.4 fusion.70
  1126.1 4.4 fusion.66
  1134.4 4.4 fusion.68
  1141.0 4.7 fusion.82
  1157.4 5.4 copy.91
  1162.8 15.7 %add_select_fusion = f32[1024,1024]{0,1:T(8,128)} fusion(f32[1024,1024]{0,1:T(8,128)} %copy-done.4, f32[1024]{0:T(1024)S(1)} %copy-done.80, pred[1024]{0:T(1024)(128)(4,1)S(1)} %copy-done.72, bf16[1024,4096]{1,0:T(8,128)(2,1)} %get-tuple-element.337, bf16[1024,4096]{1,0:T(8,128)(2,1)} %all-gather.20.cloned.1.call-done), kind=kOutput, calls=%fused_computation.100 | convolution fusion | flops 8593080320 | bytes 25170944 | tf_op jit(solution)/shard_map/dot_general | solution.py:44
  1178.6 5.4 copy.90
  1184.2 39.8 %all-reduce = (f32[1024]{0:T(1024)}, f32[1024]{0:T(1024)}, f32[1024]{0:T(1024)}, f32[1024]{0:T(1024)}, f32[16]{0:T(128)}, /*index=5*/f32[1024]{0:T(1024)}, f32[1...) all-reduce(f32[1024]{0:T(1024)S(1)} %get-tuple-element.263, ...), channel_id=1, replica_groups=mesh['rows'=4,'ffn'=8] {'rows','ffn'}, use_global_device_ids=true, to_apply=%region_24.25 | all-reduce | flops 10256 | bytes 82048 | tf_op jit(solution)/shard_map/psum | solution.py:255
  1225.8 10.6 all-reduce.1
  1240.0 22.9 %reduce-scatter.12.cloned.1.call-done = f32[32,1024]{1,0:T(8,128)} async-done(((f32[1024,1024]{1,0:T(8,128)}), f32[32,1024]{1,0:T(8,128)}) %reduce-scatter.12.cloned.1.call-update) | async-done | bytes 131088 | tf_op jit(solution)/shard_map/reduce_scatter | solution.py:250
  1262.9 142.4 %reduce-scatter.16.cloned.1.call-done = f32[32,1024]{1,0:T(8,128)} async-done(((f32[1024,1024]{1,0:T(8,128)}), f32[32,1024]{1,0:T(8,128)}) %reduce-scatter.16.cloned.1.call-update) | async-done | bytes 131088 | tf_op jit(solution)/shard_map/reduce_scatter | solution.py:252
  1405.3 142.4 %reduce-scatter.14.cloned.1.call-done = f32[32,1024]{1,0:T(8,128)} async-done(((f32[1024,1024]{1,0:T(8,128)}), f32[32,1024]{1,0:T(8,128)}) %reduce-scatter.14.cloned.1.call-update) | async-done | bytes 131088 | tf_op jit(solution)/shard_map/reduce_scatter | solution.py:251
  (312 shorter events, 106.5 us)
Async XLA Ops:
  7.2 32.0 %all-gather.14.cloned.1.call-start = ((), (), s32[]{:S(2)}) async-start(), calls=%async_computation.12 | async-start | bytes 1310720 | tf_op jit(solution)/shard_map/all_gather | solution.py:174
  7.9 87.7 %all-gather.18.cloned.1.call-start = ((), (), s32[]{:S(2)}) async-start(), calls=%async_computation.14 | async-start | bytes 1310720 | tf_op jit(solution)/shard_map/all_gather | solution.py:175
  8.7 124.7 %all-gather.10.cloned.1.call-start = ((), (), s32[]{:S(2)}) async-start(), calls=%async_computation.10 | async-start | bytes 2162688 | tf_op jit(solution)/shard_map/all_gather | solution.py:152
  9.4 182.2 %all-gather.8.cloned.1.call-start = ((), (), s32[]{:S(2)}) async-start(), calls=%async_computation.9 | async-start | bytes 2162688 | tf_op jit(solution)/shard_map/all_gather | solution.py:150
  10.0 383.6 %all-gather.12.cloned.1.call-start = ((), (), s32[]{:S(2)}) async-start(), calls=%async_computation.11 | async-start | bytes 2162688 | tf_op jit(solution)/shard_map/all_gather | solution.py:153
  10.6 397.5 %all-gather.16.cloned.1.call-start = ((), (), s32[]{:S(2)}) async-start(), calls=%async_computation.13 | async-start | bytes 9437184 | tf_op jit(solution)/shard_map/all_gather | solution.py:178
  39.3 420.0 %all-gather.20.cloned.1.call-start = ((), (), s32[]{:S(2)}) async-start(), calls=%async_computation.15 | async-start | bytes 9437184 | tf_op jit(solution)/shard_map/all_gather | solution.py:179
  39.3 5.9 collective-permute-start
  45.2 37.9 %copy-start.26 = (bf16[32,1024]{1,0:T(8,128)(2,1)}, bf16[32,1024]{1,0:T(8,128)(2,1)S(1)}, u32[]{:S(2)}) copy-start(bf16[32,1024]{1,0:T(8,128)(2,1)S(1)} %collective-permute-done) | copy-start | bytes 196612
  46.1 5.0 collective-permute-start.1
  52.0 36.0 %copy-start.69 = (f32[16]{0:T(128)S(1)}, f32[16]{0:T(128)}, u32[]{:S(2)}) copy-start(f32[16]{0:T(128)} %param.37) | copy-start | bytes 196
  52.0 15.1 collective-permute-start.2
  68.0 14.0 collective-permute-start.3
  83.1 26.0 %collective-permute-start.4 = (bf16[512,1024]{1,0:T(8,128)(2,1)}, bf16[512,1024]{1,0:T(8,128)(2,1)S(1)}, u32[]{:S(2)}, u32[]{:S(2)}) collective-permute-start(bf16[512,1024]{1,0:T(8,128)(2,1)} %get-tuple-element.339), channel_id=1, source_target_pairs={{0,16},{1,17},{2,18},{3,19},{4,20},{5,21},{6,22},{7,23},{8,24},{9,... | collective-permute-start | bytes 3145736 | tf_op jit(solution)/shard_map/ppermute | solution.py:15
  88.0 7.1 copy-start.9
  94.4 97.2 %copy-start.38 = (f32[1024]{0:T(1024)}, f32[1024]{0:T(1024)S(1)}, u32[]{:S(2)}) copy-start(f32[1024]{0:T(1024)S(1)} %broadcast_multiply_fusion.5) | copy-start | bytes 12292
  95.6 21.8 %copy-start.56 = (f32[1024]{0:T(1024)S(1)}, f32[1024]{0:T(1024)}, u32[]{:S(2)}) copy-start(f32[1024]{0:T(1024)} %param.30) | copy-start | bytes 12292
  95.6 21.8 %copy-start.78 = (f32[1024]{0:T(1024)S(1)}, f32[1024]{0:T(1024)}, u32[]{:S(2)}) copy-start(f32[1024]{0:T(1024)} %param.31) | copy-start | bytes 12292
  95.6 96.0 %copy-start.44 = (f32[1024]{0:T(1024)}, f32[1024]{0:T(1024)S(1)}, u32[]{:S(2)}) copy-start(f32[1024]{0:T(1024)S(1)} %fusion.54) | copy-start | bytes 12292
  95.7 599.2 %reduce-scatter.20.cloned.1.call-start = ((), (), s32[]{:S(2)}) async-start(), calls=%async_computation.20 | async-start | bytes 18874368 | tf_op jit(solution)/shard_map/reduce_scatter | solution.py:209
  95.7 21.7 %copy-start.10 = (bf16[1024,1024]{0,1:T(8,128)(2,1)S(1)}, bf16[1024,1024]{0,1:T(8,128)(2,1)}, u32[]{:S(2)}) copy-start(bf16[1024,1024]{0,1:T(8,128)(2,1)} %copy-done.9) | copy-start | bytes 6291460
  117.4 16.0 %copy-start.76 = (f32[1024]{0:T(1024)S(1)}, f32[1024]{0:T(1024)}, u32[]{:S(2)}) copy-start(f32[1024]{0:T(1024)} %param.36) | copy-start | bytes 12292
  122.0 69.6 %copy-start.77 = (f32[1024]{0:T(1024)S(1)}, f32[1024]{0:T(1024)}, u32[]{:S(2)}) copy-start(f32[1024]{0:T(1024)} %param.33) | copy-start | bytes 12292
  139.6 58.2 %copy-start.81 = (s32[2]{0:T(128)S(1)}, s32[2]{0:T(128)}, u32[]{:S(2)}) copy-start(s32[2]{0:T(128)} %iota_multiply_fusion) | copy-start | bytes 28
  218.9 15.7 %copy-start.7 = (bf16[1024,16,64]{0,2,1:T(8,128)(2,1)S(1)}, bf16[1024,16,64]{0,2,1:T(8,128)(2,1)}, u32[]{:S(2)}) copy-start(bf16[1024,16,64]{0,2,1:T(8,128)(2,1)} %get-tuple-element.518) | copy-start | bytes 6291460 | tf_op jit(solution)/shard_map/while
  313.0 15.8 %copy-start.7 = (bf16[1024,16,64]{0,2,1:T(8,128)(2,1)S(1)}, bf16[1024,16,64]{0,2,1:T(8,128)(2,1)}, u32[]{:S(2)}) copy-start(bf16[1024,16,64]{0,2,1:T(8,128)(2,1)} %get-tuple-element.518) | copy-start | bytes 6291460 | tf_op jit(solution)/shard_map/while
  387.5 6.1 copy-start.1
  387.5 6.1 copy-start.36
  387.5 6.0 copy-start.65
  408.0 51.2 %copy-start.18 = (bf16[1024,1024]{0,1:T(8,128)(2,1)S(1)}, bf16[1024,1024]{0,1:T(8,128)(2,1)}, u32[]{:S(2)}) copy-start(bf16[1024,1024]{0,1:T(8,128)(2,1)} %copy.83) | copy-start | bytes 6291460
  408.0 51.3 %copy-start.54 = (f32[4096]{0:T(1024)S(1)}, f32[4096]{0:T(1024)}, u32[]{:S(2)}) copy-start(f32[4096]{0:T(1024)} %param.46) | copy-start | bytes 49156
  408.0 51.3 %copy-start.71 = (pred[1024]{0:T(1024)(128)(4,1)S(1)}, pred[1024]{0:T(1024)(128)(4,1)}, u32[]{:S(2)}) copy-start(pred[1024]{0:T(1024)(128)(4,1)} %iota_compare_fusion.4) | copy-start | bytes 3076
  459.3 22.7 %copy-start.55 = (f32[4096]{0:T(1024)S(1)}, f32[4096]{0:T(1024)}, u32[]{:S(2)}) copy-start(f32[4096]{0:T(1024)} %param.47) | copy-start | bytes 49156
  482.0 30.3 %copy-start.5 = (f32[1024,1024]{0,1:T(8,128)S(1)}, f32[1024,1024]{0,1:T(8,128)}, u32[]{:S(2)}) copy-start(f32[1024,1024]{0,1:T(8,128)} %copy-done.4) | copy-start | bytes 12582916
  482.0 30.2 %copy-start.29 = (f32[1024]{0:T(1024)S(1)}, f32[1024]{0:T(1024)}, u32[]{:S(2)}) copy-start(f32[1024]{0:T(1024)} %copy-done.28) | copy-start | bytes 12292
  482.0 30.2 %copy-start.33 = (f32[1024]{0:T(1024)S(1)}, f32[1024]{0:T(1024)}, u32[]{:S(2)}) copy-start(f32[1024]{0:T(1024)} %param.42) | copy-start | bytes 12292
  482.0 30.2 %copy-start.35 = (f32[1024]{0:T(1024)S(1)}, f32[1024]{0:T(1024)}, u32[]{:S(2)}) copy-start(f32[1024]{0:T(1024)} %copy-done.34) | copy-start | bytes 12292
  482.0 30.2 %copy-start.64 = (f32[1024]{0:T(1024)S(1)}, f32[1024]{0:T(1024)}, u32[]{:S(2)}) copy-start(f32[1024]{0:T(1024)} %param.43) | copy-start | bytes 12292
  527.5 336.3 %reduce-scatter.24.cloned.1.call-start = ((), (), s32[]{:S(2)}) async-start(), calls=%async_computation.22 | async-start | bytes 18874368 | tf_op jit(solution)/shard_map/reduce_scatter | solution.py:210
  542.0 682.0 %reduce-scatter.28.cloned.1.call-start = ((), (), s32[]{:S(2)}) async-start(), calls=%async_computation.24 | async-start | bytes 2359296
  569.6 666.8 %reduce-scatter.22.cloned.1.call-start = ((), (), s32[]{:S(2)}) async-start(), calls=%async_computation.21 | async-start | bytes 1310720 | tf_op jit(solution)/shard_map/reduce_scatter | solution.py:214
  697.6 540.6 %reduce-scatter.26.cloned.1.call-start = ((), (), s32[]{:S(2)}) async-start(), calls=%async_computation.23 | async-start | bytes 1310720 | tf_op jit(solution)/shard_map/reduce_scatter | solution.py:217
  697.7 6.7 copy-start.14
  704.4 6.5 copy-start.49
  866.5 373.5 %reduce-scatter.18.cloned.1.call-start = ((), (), s32[]{:S(2)}) async-start(), calls=%async_computation.19 | async-start | bytes 4325376 | tf_op jit(solution)/shard_map/reduce_scatter | solution.py:253
  880.2 382.7 %reduce-scatter.12.cloned.1.call-start = ((), (), s32[]{:S(2)}) async-start(), calls=%async_computation.16 | async-start | bytes 4325376 | tf_op jit(solution)/shard_map/reduce_scatter | solution.py:250
  884.7 19.0 %copy-start.8 = (bf16[1024,16,64]{0,2,1:T(8,128)(2,1)S(1)}, bf16[1024,16,64]{0,2,1:T(8,128)(2,1)}, u32[]{:S(2)}) copy-start(bf16[1024,16,64]{0,2,1:T(8,128)(2,1)} %get-tuple-element.560) | copy-start | bytes 6291460 | tf_op jit(solution)/shard_map/while
  884.7 19.0 %copy-start.17 = (bf16[1024,16,64]{0,2,1:T(8,128)(2,1)S(1)}, bf16[1024,16,64]{0,2,1:T(8,128)(2,1)}, u32[]{:S(2)}) copy-start(bf16[1024,16,64]{0,2,1:T(8,128)(2,1)} %get-tuple-element.559) | copy-start | bytes 6291460 | tf_op jit(solution)/shard_map/while
  957.9 12.3 copy-start
  977.9 18.1 %copy-start.3 = (bf16[1024,16,64]{0,2,1:T(8,128)(2,1)S(1)}, bf16[1024,16,64]{0,2,1:T(8,128)(2,1)}, u32[]{:S(2)}) copy-start(bf16[1024,16,64]{0,2,1:T(8,128)(2,1)} %get-tuple-element.595) | copy-start | bytes 6291460 | tf_op jit(solution)/shard_map/while
  998.5 18.8 %copy-start.8 = (bf16[1024,16,64]{0,2,1:T(8,128)(2,1)S(1)}, bf16[1024,16,64]{0,2,1:T(8,128)(2,1)}, u32[]{:S(2)}) copy-start(bf16[1024,16,64]{0,2,1:T(8,128)(2,1)} %get-tuple-element.560) | copy-start | bytes 6291460 | tf_op jit(solution)/shard_map/while
  998.5 18.8 %copy-start.17 = (bf16[1024,16,64]{0,2,1:T(8,128)(2,1)S(1)}, bf16[1024,16,64]{0,2,1:T(8,128)(2,1)}, u32[]{:S(2)}) copy-start(bf16[1024,16,64]{0,2,1:T(8,128)(2,1)} %get-tuple-element.559) | copy-start | bytes 6291460 | tf_op jit(solution)/shard_map/while
  1071.2 13.6 copy-start
  1092.6 19.2 %copy-start.3 = (bf16[1024,16,64]{0,2,1:T(8,128)(2,1)S(1)}, bf16[1024,16,64]{0,2,1:T(8,128)(2,1)}, u32[]{:S(2)}) copy-start(bf16[1024,16,64]{0,2,1:T(8,128)(2,1)} %get-tuple-element.595) | copy-start | bytes 6291460 | tf_op jit(solution)/shard_map/while
  1111.9 5.8 copy-start.12
  1112.0 5.8 copy-start.39
  1112.0 5.8 copy-start.45
  1112.0 5.8 copy-start.57
  1112.0 5.8 copy-start.79
  1122.2 283.1 %reduce-scatter.16.cloned.1.call-start = ((), (), s32[]{:S(2)}) async-start(), calls=%async_computation.18 | async-start | bytes 4325376 | tf_op jit(solution)/shard_map/reduce_scatter | solution.py:252
  1130.5 417.1 %reduce-scatter.14.cloned.1.call-start = ((), (), s32[]{:S(2)}) async-start(), calls=%async_computation.17 | async-start | bytes 4325376 | tf_op jit(solution)/shard_map/reduce_scatter | solution.py:251
  1178.6 5.6 copy-start.59
  1178.6 5.6 copy-start.60
  1178.6 5.6 copy-start.61
  (45 other events, 145.5 us)
Sparse Core Ops, SparseCore 0:
  9.9 29.3 all-gather.13
  41.1 28.0 all-gather.17
  72.1 61.2 all-gather.9
  136.2 55.3 all-gather.7
  194.4 55.3 all-gather.11
  251.3 80.9 all-gather.15
  333.8 80.6 all-gather.19
  527.7 167.1 reduce-scatter.19
  697.2 166.5 reduce-scatter.23
  866.0 34.2 reduce-scatter.27
  903.1 26.1 reduce-scatter.21
  932.3 27.7 reduce-scatter.25
  962.9 142.5 reduce-scatter.17
  1122.3 140.5 reduce-scatter.11
  1265.6 139.6 reduce-scatter.15
  1408.0 139.6 reduce-scatter.13
